TPU v7x, 32 devices: a whole 2x2x4 slice. The times are simulated.
32 devices in a mesh: seq: 4 (over y, x), grp: 2 (over core), wsh: 4 (over z).
Axes of the slice: x: 2, y: 2, z: 4, core: 2. Of those that a mesh axis runs over, the one named last changes fastest.
Arguments:
- hidden: bfloat16 [8, 1024, 1536], P(('grp', 'wsh'), 'seq'), may hold values from -6 to 6
- norm_gain: bfloat16 [1536], P('wsh'), may hold values from 0.5 to 1.5
- in_weight: bfloat16 [1536, 6448], P('wsh'), may hold values from -0.15625 to 0.15625
- conv_weight: bfloat16 [3328, 4], P('wsh'), may hold values from -3 to 3
- conv_bias: bfloat16 [3328], P('wsh'), may hold values from -3 to 3
- dt_bias: bfloat16 [48], P('wsh'), may hold values from -13 to -3
- a_log: bfloat16 [48], P('wsh'), may hold values from 0 to 2.7
- skip_gain: bfloat16 [48], P('wsh'), may hold values from 0.5 to 2
- gate_gain: bfloat16 [3072], P('wsh'), may hold values from 0.5 to 1.5
- out_weight: bfloat16 [3072, 1536], P('wsh'), may hold values from -0.109375 to 0.109375
- d_out: bfloat16 [8, 1024, 1536], P(('grp', 'wsh'), 'seq'), may hold values from -6 to 6
Outputs:
- layer_out: bfloat16 [8, 1024, 1536], P(('grp', 'wsh'), 'seq')
- d_hidden: bfloat16 [8, 1024, 1536], P(('grp', 'wsh'), 'seq')
- grad_norm_gain: float32 [1536], P('wsh')
- grad_in_weight: float32 [1536, 6448], P('wsh')
- grad_conv_weight: float32 [3328, 4], P('wsh')
- grad_conv_bias: float32 [3328], P('wsh')
- grad_dt_bias: float32 [48], P('wsh')
- grad_a_log: float32 [48], P('wsh')
- grad_skip_gain: float32 [48], P('wsh')
- grad_gate_gain: float32 [3072], P('wsh')
- grad_out_weight: float32 [3072, 1536], P('wsh')
All inputs are finite; a program needn't handle non-finite values.
Results may differ from a plain program's by a relative error of at most 0.0091.
Values may be sent and summed in bfloat16 or wider, within the bound.
No kernel may reach another device: no remote copies, remote signals or barrier semaphores. Data moves between devices by JAX's collectives and lax.ppermute only.
A program may use at most 320 MiB of HBM per device.

v0:
```python
import jax
import jax.numpy as jnp
from jax import lax
from jax.sharding import PartitionSpec as P

DI = 3072
KCONV = 4
QCH = 256
CONVC = 3328
epsilon = 1e-05
highest = lax.Precision.HIGHEST


def shifted(block, axis, distance):
    devices = range(lax.axis_size(axis))
    route = [(i - distance, i) for i in devices if i - distance in devices]
    return lax.ppermute(block, axis, route)


def rms_apply(values, gain_vec):
    inverse = lax.rsqrt(jnp.mean(values * values, axis=-1, keepdims=True) + epsilon)
    return values * inverse * gain_vec[None, :]


def gated_apply(mixer_out, gate_in, gain_vec):
    product = mixer_out * jax.nn.silu(gate_in)
    inverse = lax.rsqrt(jnp.mean(product * product, axis=-1, keepdims=True) + epsilon)
    return product * inverse * gain_vec[None, :]


def conv_apply(padded, weight, bias_vec):
    tap_count = weight.shape[1]
    row_count = padded.shape[0] - tap_count + 1
    summed = jnp.zeros((row_count, padded.shape[1]), jnp.float32) + bias_vec[None, :]
    for offset in range(tap_count):
        summed = summed + padded[offset : offset + row_count] * weight[:, offset][None, :]
    return jax.nn.silu(summed)


def ssd_apply(x_values, dt_raw, b_and_c, dt_bias, a_log, skip_gain):
    length, head_count = dt_raw.shape
    head_size = x_values.shape[1] // head_count
    state_count = b_and_c.shape[1] // 2
    block_count = length // QCH
    dt_value = jax.nn.softplus(dt_raw + dt_bias[None, :])
    log_rate = -jnp.exp(a_log)[None, :] * dt_value
    causal = (jnp.arange(QCH)[:, None] >= jnp.arange(QCH)[None, :]).astype(jnp.float32)
    x_blocks = x_values.reshape(block_count, QCH, head_count, head_size)
    dt_blocks = dt_value.reshape(block_count, QCH, head_count)
    rate_blocks = log_rate.reshape(block_count, QCH, head_count)
    b_blocks = b_and_c[:, :state_count].reshape(block_count, QCH, state_count)
    c_blocks = b_and_c[:, state_count:].reshape(block_count, QCH, state_count)

    def advance(carried, pieces):
        x_block, dt_block, rate_block, b_block, c_block = pieces
        cumulated = jnp.cumsum(rate_block, axis=0)
        gram_matrix = jnp.dot(c_block, b_block.T, precision=highest)
        spread = cumulated.T[:, :, None] - cumulated.T[:, None, :]
        mixing = (
            jnp.exp(spread * causal[None])
            * causal[None]
            * gram_matrix[None]
            * dt_block.T[:, None, :]
        )
        result = jnp.einsum("hts,shp->thp", mixing, x_block, precision=highest)
        result = (
            result
            + jnp.einsum("tn,hnp->thp", c_block, carried, precision=highest)
            * jnp.exp(cumulated)[:, :, None]
        )
        final_sum = cumulated[-1]
        tail_weight = jnp.exp(final_sum[None, :] - cumulated) * dt_block
        carried = carried * jnp.exp(final_sum)[:, None, None] + jnp.einsum(
            "sn,sh,shp->hnp", b_block, tail_weight, x_block, precision=highest
        )
        return (carried, result)

    initial = jnp.zeros((head_count, state_count, head_size), jnp.float32)
    _, outputs = lax.scan(advance, initial, (x_blocks, dt_blocks, rate_blocks, b_blocks, c_blocks))
    return (
        outputs.reshape(length, head_count * head_size)
        + x_values * jnp.repeat(skip_gain, head_size)[None, :]
    )


def reduce_grads(grads):
    shares = (
        lax.psum_scatter(grads[0], "wsh", scatter_dimension=0, tiled=True),
        lax.psum_scatter(grads[1], "wsh", scatter_dimension=0, tiled=True),
        lax.psum_scatter(grads[2], "wsh", scatter_dimension=0, tiled=True),
        lax.psum_scatter(grads[3], "wsh", scatter_dimension=0, tiled=True),
        lax.psum_scatter(grads[4], "wsh", scatter_dimension=0, tiled=True),
        lax.psum_scatter(grads[5], "wsh", scatter_dimension=0, tiled=True),
        lax.psum_scatter(grads[6], "wsh", scatter_dimension=0, tiled=True),
        lax.psum_scatter(grads[7], "wsh", scatter_dimension=0, tiled=True),
        lax.psum_scatter(grads[8], "wsh", scatter_dimension=0, tiled=True),
    )
    return lax.psum(
        (
            shares[0],
            shares[1],
            shares[2],
            shares[3],
            shares[4],
            shares[5],
            shares[6],
            shares[7],
            shares[8],
        ),
        ("seq", "grp"),
    )


def body(
    hidden,
    norm_gain,
    in_weight,
    conv_weight,
    conv_bias,
    dt_bias,
    a_log,
    skip_gain,
    gate_gain,
    out_weight,
    d_out,
):
    gathered = (
        lax.all_gather(norm_gain, "wsh", axis=0, tiled=True),
        lax.all_gather(in_weight, "wsh", axis=0, tiled=True),
        lax.all_gather(conv_weight, "wsh", axis=0, tiled=True),
        lax.all_gather(conv_bias, "wsh", axis=0, tiled=True),
        lax.all_gather(dt_bias, "wsh", axis=0, tiled=True),
        lax.all_gather(a_log, "wsh", axis=0, tiled=True),
        lax.all_gather(skip_gain, "wsh", axis=0, tiled=True),
    )
    full_norm, full_in, full_conv, full_cbias, full_dtb, full_alog, full_skip = gathered
    tokens_f = hidden[0].astype(jnp.float32)
    cotangent = d_out[0]
    normed_f, rms_back = jax.vjp(rms_apply, tokens_f, full_norm.astype(jnp.float32))
    normed = lax.optimization_barrier(normed_f.astype(jnp.bfloat16))
    projected = lax.optimization_barrier(
        jnp.dot(normed, full_in, preferred_element_type=jnp.float32).astype(jnp.bfloat16)
    )
    gate_part = projected[:, :DI]
    conv_input = projected[:, DI : DI + CONVC]
    dt_part = projected[:, DI + CONVC :]
    rim_rows = shifted(conv_input[conv_input.shape[0] - (KCONV - 1) :], "seq", 1)
    padded = jnp.concatenate([rim_rows, conv_input], axis=0).astype(jnp.float32)
    conved_f, conv_back = jax.vjp(
        conv_apply, padded, full_conv.astype(jnp.float32), full_cbias.astype(jnp.float32)
    )
    conved = lax.optimization_barrier(conved_f.astype(jnp.bfloat16))
    x_heads, dt_heads = (
        lax.all_to_all(conved[:, :DI], "seq", split_axis=1, concat_axis=0, tiled=True),
        lax.all_to_all(dt_part, "seq", split_axis=1, concat_axis=0, tiled=True),
    )
    bc_whole = lax.all_gather(conved[:, DI:], "seq", axis=0, tiled=True)
    local_heads = dt_heads.shape[1]
    head_start = lax.axis_index("seq") * local_heads
    bias_local = lax.dynamic_slice_in_dim(full_dtb.astype(jnp.float32), head_start, local_heads)
    alog_local = lax.dynamic_slice_in_dim(full_alog.astype(jnp.float32), head_start, local_heads)
    skip_local = lax.dynamic_slice_in_dim(full_skip.astype(jnp.float32), head_start, local_heads)
    x_float = x_heads.astype(jnp.float32)
    dt_float = dt_heads.astype(jnp.float32)
    bc_float = bc_whole.astype(jnp.float32)
    y_heads = ssd_apply(x_float, dt_float, bc_float, bias_local, alog_local, skip_local).astype(
        jnp.bfloat16
    )
    y_tokens = lax.all_to_all(y_heads, "seq", split_axis=0, concat_axis=1, tiled=True)
    full_gate, full_out = (
        lax.all_gather(gate_gain, "wsh", axis=0, tiled=True),
        lax.all_gather(out_weight, "wsh", axis=0, tiled=True),
    )
    gated_f, gate_back = jax.vjp(
        gated_apply,
        y_tokens.astype(jnp.float32),
        gate_part.astype(jnp.float32),
        full_gate.astype(jnp.float32),
    )
    gated = gated_f.astype(jnp.bfloat16)
    layer_out = (tokens_f + jnp.dot(gated, full_out, preferred_element_type=jnp.float32)).astype(
        jnp.bfloat16
    )
    grad_out = jnp.einsum("td,te->de", gated, cotangent, preferred_element_type=jnp.float32)
    d_gated = lax.dot_general(
        cotangent, full_out, (((1,), (1,)), ((), ())), preferred_element_type=jnp.float32
    )
    d_mixer, d_gate_part, grad_gate = gate_back(d_gated)
    d_y_heads = lax.all_to_all(
        d_mixer.astype(jnp.bfloat16), "seq", split_axis=1, concat_axis=0, tiled=True
    )
    _, ssd_back = jax.vjp(
        ssd_apply, x_float, dt_float, bc_float, bias_local, alog_local, skip_local
    )
    d_x, d_dt, d_bc_part, grad_dtb, grad_alog, grad_skip = ssd_back(d_y_heads.astype(jnp.float32))
    d_bc = lax.psum_scatter(d_bc_part, "seq", scatter_dimension=0, tiled=True)
    d_x_tokens, d_dt_tokens = (
        lax.all_to_all(d_x.astype(jnp.bfloat16), "seq", split_axis=0, concat_axis=1, tiled=True),
        lax.all_to_all(d_dt.astype(jnp.bfloat16), "seq", split_axis=0, concat_axis=1, tiled=True),
    )
    d_conved = jnp.concatenate([d_x_tokens.astype(jnp.float32), d_bc], axis=1)
    d_padded, grad_conv, grad_cbias = conv_back(d_conved)
    rim_grad = shifted(d_padded[: KCONV - 1].astype(jnp.bfloat16), "seq", -1).astype(jnp.float32)
    own_rows = conv_input.shape[0]
    d_conv_input = d_padded[KCONV - 1 :] + jnp.concatenate(
        [jnp.zeros((own_rows - (KCONV - 1), CONVC), jnp.float32), rim_grad], axis=0
    )
    d_projected = jnp.concatenate(
        [d_gate_part, d_conv_input, d_dt_tokens.astype(jnp.float32)], axis=1
    ).astype(jnp.bfloat16)
    grad_in = jnp.einsum("td,tp->dp", normed, d_projected, preferred_element_type=jnp.float32)
    d_normed = lax.dot_general(
        d_projected, full_in, (((1,), (1,)), ((), ())), preferred_element_type=jnp.float32
    )
    d_tokens, grad_norm = rms_back(d_normed)
    d_hidden = (cotangent.astype(jnp.float32) + d_tokens).astype(jnp.bfloat16)
    all_heads = full_dtb.shape[0]
    placed_dtb = lax.dynamic_update_slice_in_dim(
        jnp.zeros((all_heads,), jnp.float32), grad_dtb, head_start, 0
    )
    placed_alog = lax.dynamic_update_slice_in_dim(
        jnp.zeros((all_heads,), jnp.float32), grad_alog, head_start, 0
    )
    placed_skip = lax.dynamic_update_slice_in_dim(
        jnp.zeros((all_heads,), jnp.float32), grad_skip, head_start, 0
    )
    reduced = reduce_grads(
        (
            grad_norm,
            grad_in,
            grad_conv,
            grad_cbias,
            placed_dtb,
            placed_alog,
            placed_skip,
            grad_gate,
            grad_out,
        )
    )
    return (
        layer_out[None],
        d_hidden[None],
        reduced[0],
        reduced[1],
        reduced[2],
        reduced[3],
        reduced[4],
        reduced[5],
        reduced[6],
        reduced[7],
        reduced[8],
    )


def solution(mesh):
    placed = (
        P(("grp", "wsh"), "seq", None),
        P("wsh"),
        P("wsh", None),
        P("wsh", None),
        P("wsh"),
        P("wsh"),
        P("wsh"),
        P("wsh"),
        P("wsh"),
        P("wsh", None),
        P(("grp", "wsh"), "seq", None),
    )
    return jax.shard_map(
        body,
        mesh=mesh,
        in_specs=placed,
        out_specs=(
            P(("grp", "wsh"), "seq", None),
            P(("grp", "wsh"), "seq", None),
            P("wsh"),
            P("wsh", None),
            P("wsh", None),
            P("wsh"),
            P("wsh"),
            P("wsh"),
            P("wsh"),
            P("wsh"),
            P("wsh", None),
        ),
        check_vma=False,
    )
```

profile of v0, /device:TPU:0, one launch (start us, length us, event | category | flops | bytes accessed | tf_op | source)
XLA Modules:
  0.0 2245.3 jit_solution(12582450332125656297)
XLA Ops:
  9.0 13.6 all-gather
  22.7 13.5 all-gather.1
  37.5 312.8 %all-gather.6.cloned.1.call-done = bf16[1536,6448]{0,1:T(8,128)(2,1)} async-done(((bf16[384,6448]{0,1:T(8,128)(2,1)}), bf16[1536,6448]{0,1:T(8,128)(2,1)}) %all-gather.6.cloned.1.call-update) | async-done | bytes 19808272 | tf_op jit(solution)/shard_map/all_gather | solution.py:129
  350.3 10.3 convolution_convert_fusion
  363.9 3.2 collective-permute-start
  370.2 10.7 all-reduce.25
  382.9 3.6 all-to-all-start
  389.6 6.9 multiply_convert_fusion
  397.8 4.4 all-to-all-start.1
  404.4 26.2 %all_gather.36 = bf16[1024,256]{0,1:T(8,128)(2,1)S(1)} all-gather(bf16[256,256]{0,1:T(8,128)(2,1)S(1)} %slice.146), channel_id=1, replica_groups=mesh['seq'=4,'grp'=2,'wsh'=4] {'seq'}, dimensions={0}, use_global_device_ids=true | all-gather | bytes 655360 | tf_op jit(solution)/shard_map/all_gather | solution.py:157
  436.7 52.1 %while.86 = (s32[]{:T(128)}, f32[12,128,64]{1,2,0:T(8,128)}, f32[4,256,12,64]{1,3,2,0:T(8,128)}, f32[4,256,12]{1,2,0:T(8,128)}, f32[4,256,12]{1,2,0:T(8,128)S(1)...) while((s32[]{:T(128)}, f32[12,128,64]{1,2,0:T(8,128)}, ...), condition=%wide.region_4.5_spmd.clone.clone, body=%wide.region_1.4_spmd.clone.clone.sunk | while | flops 1313970176 | bytes 8233615 | solution.py:79
  444.2 4.7 fusion.259
  457.5 4.8 fusion.259
  470.7 4.7 fusion.259
  484.0 4.7 fusion.259
  488.7 4.0 fusion.162
  492.7 4.5 all-to-all-start.2
  497.3 19.0 all-gather.2
  516.3 4.6 multiply_reduce_fusion.7
  521.5 8.7 multiply_reduce_fusion.4
  530.3 5.1 fusion.160
  535.4 4.3 all-to-all-start.3
  545.9 128.5 %while.87 = (s32[]{:T(128)}, f32[12,128,64]{1,2,0:T(8,128)}, f32[4,128,256]{1,2,0:T(8,128)}, f32[4,12,256,256]{3,2,1,0:T(8,128)}, f32[4,1,256,256]{3,2,1,0:T(8,1...) while((s32[]{:T(128)}, f32[12,128,64]{1,2,0:T(8,128)}, ...), condition=%wide.region_10.11_spmd.clone.clone, body=%wide.region_7.10_spmd.clone.clone.sunk | while | flops 709793792 | bytes 22214624 | solution.py:79
  572.1 5.3 multiply_dynamic-update-slice_fusion.3
  604.6 5.1 multiply_dynamic-update-slice_fusion.3
  636.9 5.1 multiply_dynamic-update-slice_fusion.3
  669.1 5.2 multiply_dynamic-update-slice_fusion.3
  674.3 3.3 convert_element_type.189
  682.6 290.8 %while.88 = (s32[]{:T(128)}, f32[12,128,64]{1,2,0:T(8,128)S(1)}, f32[4,256,12,64]{1,3,2,0:T(8,128)}, f32[4,256,12]{1,2,0:T(8,128)}, f32[4,256,12]{1,2,0:T(8,128)...) while((s32[]{:T(128)}, f32[12,128,64]{1,2,0:T(8,128)S(1)}, ...), condition=%wide.region_21.22_spmd.clone.clone, body=%wide.region_11.21_spmd.clone.clone.sunk | while | flops 2628807680 | bytes 29113356 | solution.py:79
  701.0 3.3 convolution_bitcast_fusion.8
  704.3 3.2 convolution_bitcast_fusion.7
  708.5 9.3 fusion.282
  736.6 3.8 reduce-window.64
  750.1 5.3 fusion.281
  773.6 3.3 convolution_bitcast_fusion.8
  776.9 3.2 convolution_bitcast_fusion.7
  781.1 9.3 fusion.282
  809.1 3.8 reduce-window.64
  822.7 5.3 fusion.281
  846.2 3.3 convolution_bitcast_fusion.8
  849.5 3.2 convolution_bitcast_fusion.7
  853.7 9.3 fusion.282
  881.7 3.8 reduce-window.64
  895.3 5.2 fusion.281
  918.8 3.3 convolution_bitcast_fusion.8
  922.1 3.2 convolution_bitcast_fusion.7
  926.3 9.4 fusion.282
  954.5 3.8 reduce-window.64
  968.0 5.2 fusion.281
  980.1 9.4 fusion.176
  992.9 24.3 %all_to_all.69 = bf16[4,256,768]{1,2,0:T(8,128)(2,1)S(1)} all-to-all(bf16[4,256,768]{1,2,0:T(8,128)(2,1)S(1)} %fusion.161), channel_id=1, replica_groups=mesh['seq'=4,'grp'=2,'wsh'=4] {'seq'}, dimensions={0} | all-to-all | bytes 3145728 | tf_op jit(solution)/shard_map/all_to_all | solution.py:198
  1019.2 12.2 multiply_reduce_fusion.3
  1033.9 4.2 pad_add_fusion
  1044.5 9.7 all_to_all.70
  1055.6 4.9 fusion.154
  1060.5 19.0 fusion.173
  1081.5 252.9 %reduce-scatter.11.cloned.1.call-done = f32[768,1536]{1,0:T(8,128)} async-done(((f32[3072,1536]{1,0:T(8,128)}), f32[768,1536]{1,0:T(8,128)}) %reduce-scatter.11.cloned.1.call-update) | async-done | bytes 4718608 | tf_op jit(solution)/shard_map/reduce_scatter | solution.py:96
  1334.4 651.6 %reduce-scatter.9.cloned.1.call-done = f32[384,6448]{0,1:T(8,128)} async-done(((f32[1536,6448]{0,1:T(8,128)}), f32[384,6448]{0,1:T(8,128)}) %reduce-scatter.9.cloned.1.call-update) | async-done | bytes 9904144 | tf_op jit(solution)/shard_map/reduce_scatter | solution.py:89
  1988.7 7.5 fusion.164
  1999.9 14.0 fusion.168
  2013.9 21.4 all-reduce.24
  2039.8 24.8 %all-reduce.22 = (f32[384]{0:T(512)}, f32[832,4]{0,1:T(4,128)}, f32[832]{0:T(1024)}, f32[12]{0:T(128)}, f32[12]{0:T(128)}, /*index=5*/f32[12]{0:T(128)}, f32[768]{0:T(1024)}) all-reduce(f32[384]{0:T(512)S(1)} %dynamic-slice.5, f32[832,4]{0,1:T(4,128)S(1)} %copy.193, ...), channel_id=1, replica_groups=mesh['seq'=4,'grp'=2,'wsh'=4] {'seq','grp'}, use_global_device_ids=true, to_apply=%region_26.27 | all-reduce | flops 5348 | bytes 42784 | tf_op jit(solution)/shard_map/psum | solution.py:98
  2064.6 163.0 %all-reduce.28.cloned.1.call-done = (f32[384,6448]{0,1:T(8,128)}, f32[768,1536]{1,0:T(8,128)}) async-done(((f32[384,6448]{0,1:T(8,128)}, f32[768,1536]{1,0:T(8,128)}), (f32[384,6448]{0,1:T(8,128)}, f32[768,1536]{1,0:T(8,128)})) %all-reduce.28.cloned.1.call-update) | async-done | bytes 14622736 | tf_op jit(solution)/shard_map/psum | solution.py:98
  2227.6 8.5 copy.389
  (580 shorter events, 399.8 us)
Async XLA Ops:
  7.2 15.5 copy-start.41
  7.2 343.1 %all-gather.6.cloned.1.call-start = ((), (), s32[]{:S(2)}) async-start(), calls=%async_computation.10 | async-start | bytes 24760320 | tf_op jit(solution)/shard_map/all_gather | solution.py:129
  7.9 513.5 %all-gather.8.cloned.1.call-start = ((), (), s32[]{:S(2)}) async-start(), calls=%async_computation.11 | async-start | bytes 11796480 | tf_op jit(solution)/shard_map/all_gather | solution.py:172
  8.9 13.7 copy-start.35
  9.0 351.7 %copy-start.37 = (f32[256]{0:T(256)}, f32[256]{0:T(256)S(1)}, u32[]{:S(2)}) copy-start(f32[256]{0:T(256)S(1)} %fusion.187) | copy-start | bytes 3076
  22.7 338.0 %copy-start.29 = (f32[1536]{0:T(1024)}, f32[1536]{0:T(1024)S(1)}, u32[]{:S(2)}) copy-start(f32[1536]{0:T(1024)S(1)} %reshape.483) | copy-start | bytes 18436
  37.5 329.9 %copy-start.46 = (u32[32]{0:T(128)S(1)}, u32[32]{0:T(128)}, u32[]{:S(2)}) copy-start(u32[32]{0:T(128)} %constant.226) | copy-start | bytes 388
  37.5 331.8 %copy-start.52 = (bf16[12]{0:T(256)(128)(2,1)S(1)}, bf16[12]{0:T(256)(128)(2,1)}, u32[]{:S(2)}) copy-start(bf16[12]{0:T(256)(128)(2,1)} %param.22) | copy-start | bytes 76
  37.5 332.0 %copy-start.53 = (bf16[12]{0:T(256)(128)(2,1)S(1)}, bf16[12]{0:T(256)(128)(2,1)}, u32[]{:S(2)}) copy-start(bf16[12]{0:T(256)(128)(2,1)} %param.23) | copy-start | bytes 76
  37.5 332.3 %copy-start.54 = (bf16[12]{0:T(256)(128)(2,1)S(1)}, bf16[12]{0:T(256)(128)(2,1)}, u32[]{:S(2)}) copy-start(bf16[12]{0:T(256)(128)(2,1)} %param.24) | copy-start | bytes 76
  37.5 332.5 %copy-start.47 = (bf16[832]{0:T(1024)(128)(2,1)S(1)}, bf16[832]{0:T(1024)(128)(2,1)}, u32[]{:S(2)}) copy-start(bf16[832]{0:T(1024)(128)(2,1)} %param.21) | copy-start | bytes 4996
  360.7 22.3 copy-start.6
  363.9 22.6 %collective-permute-start = (bf16[3,3328]{1,0:T(4,128)(2,1)S(1)}, bf16[3,3328]{1,0:T(4,128)(2,1)S(1)}, u32[]{:S(2)}, u32[]{:S(2)}) collective-permute-start(bf16[3,3328]{1,0:T(4,128)(2,1)S(1)} %copy.162), channel_id=1, source_target_pairs={{0,8},{8,16},{16,24},{1,9},{9,17},{17,25},{2,10},{10,18},{18,26},{... | collective-permute-start | bytes 59912 | tf_op jit(solution)/shard_map/ppermute | solution.py:17
  367.3 22.2 copy-start.21
  367.3 22.2 copy-start.23
  367.3 22.2 copy-start.25
  367.3 22.2 copy-start.27
  382.9 14.8 all-to-all-start
  389.5 7.0 copy-start
  397.8 5.4 copy-start.17
  397.8 35.0 %all-to-all-start.1 = ((bf16[256,4,768]{0,2,1:T(8,128)(2,1)}), bf16[256,4,768]{0,2,1:T(8,128)(2,1)}, u32[]{:S(2)}, u32[]{:S(2)}) async-start(bf16[256,4,768]{0,2,1:T(8,128)(2,1)} %bitcast.6), calls=%async_computation.1 | async-start | bytes 3145728 | tf_op jit(solution)/shard_map/all_to_all | solution.py:154
  444.2 4.8 copy-start.11
  457.4 4.8 copy-start.11
  470.7 4.8 copy-start.11
  484.0 4.7 copy-start.11
  488.7 4.0 copy-start.12
  492.7 4.6 copy-start.48
  492.7 23.6 %all-to-all-start.2 = ((bf16[4,256,768]{1,2,0:T(8,128)(2,1)}), bf16[4,256,768]{1,2,0:T(8,128)(2,1)}, u32[]{:S(2)}, u32[]{:S(2)}) async-start(bf16[4,256,768]{1,2,0:T(8,128)(2,1)} %fusion.162), calls=%async_computation.2 | async-start | bytes 3145728 | tf_op jit(solution)/shard_map/all_to_all | solution.py:169
  516.3 14.0 copy-start.15
  521.5 8.8 copy-start.31
  521.5 8.8 copy-start.40
  521.5 8.8 copy-start.1
  535.4 138.9 %all-to-all-start.3 = ((bf16[256,4,768]{0,2,1:T(8,128)(2,1)}), bf16[256,4,768]{0,2,1:T(8,128)(2,1)}, u32[]{:S(2)}, u32[]{:S(2)}) async-start(bf16[256,4,768]{0,2,1:T(8,128)(2,1)} %bitcast.595), calls=%async_computation.3 | async-start | bytes 3145728 | tf_op jit(solution)/shard_map/all_to_all | solution.py:189
  539.7 479.4 %reduce-scatter.7.cloned.1.call-start = ((), (), s32[]{:S(2)}) async-start(), calls=%async_computation.12 | async-start | bytes 1310720 | tf_op jit(solution)/shard_map/reduce_scatter | solution.py:196
  701.0 7.5 copy-start.14
  773.6 7.5 copy-start.14
  846.2 7.5 copy-start.14
  918.8 7.5 copy-start.14
  973.4 6.7 copy-start.2
  973.4 6.7 copy-start.16
  973.4 6.6 copy-start.32
  980.0 354.4 %reduce-scatter.11.cloned.1.call-start = ((), (), s32[]{:S(2)}) async-start(), calls=%async_computation.14 | async-start | bytes 23592960 | tf_op jit(solution)/shard_map/reduce_scatter | solution.py:96
  989.5 996.6 %reduce-scatter.9.cloned.1.call-start = ((), (), s32[]{:S(2)}) async-start(), calls=%async_computation.13 | async-start | bytes 49520640 | tf_op jit(solution)/shard_map/reduce_scatter | solution.py:89
  1019.2 12.2 copy-start.22
  1019.2 12.2 copy-start.24
  1019.2 12.2 copy-start.26
  1019.2 12.3 copy-start.28
  1033.8 10.4 copy-start.18
  1033.8 10.4 copy-start.19
  1033.8 10.4 copy-start.20
  1033.9 10.4 copy-start.43
  1033.9 10.4 copy-start.45
  1042.9 11.4 collective-permute-start.1
  1055.6 4.9 copy-start.8
  1079.5 959.1 %reduce-scatter.13.cloned.1.call-start = ((), (), s32[]{:S(2)}) async-start(), calls=%async_computation.15 | async-start | bytes 2129920
  1081.4 1146.1 %all-reduce.28.cloned.1.call-start = ((), (), s32[]{:S(2)}) async-start(), calls=%async_computation.16 | async-start | bytes 29245440 | tf_op jit(solution)/shard_map/psum | solution.py:98
  1996.2 3.7 copy-start.5
  1996.2 3.7 copy-start.7
  1996.2 3.7 copy-start.30
  1996.2 3.7 copy-start.38
  1999.9 14.0 copy-start.34
  1999.9 35.8 %copy-start.36 = (f32[256]{0:T(256)S(1)}, f32[256]{0:T(256)}, u32[]{:S(2)}) copy-start(f32[256]{0:T(256)} %copy-done.35) | copy-start | bytes 3076
  1999.9 35.8 %copy-start.13 = (bf16[1,256,1536]{2,1,0:T(8,128)(2,1)S(1)}, bf16[1,256,1536]{2,1,0:T(8,128)(2,1)}, u32[]{:S(2)}) copy-start(bf16[1,256,1536]{2,1,0:T(8,128)(2,1)} %param.27) | copy-start | bytes 2359300
  2227.6 8.5 copy-start.9
  (13 other events, 25.8 us)
Sparse Core Ops, SparseCore 0:
  9.6 340.6 all-gather.5
  351.9 166.4 all-gather.7
  980.1 36.9 reduce-scatter.6
  1019.4 315.0 reduce-scatter.10
  1336.6 649.3 reduce-scatter.8
  1988.8 40.4 reduce-scatter.12
  2033.1 194.4 all-reduce.27
where the time goes:
time: 2260 us; the launch traced here: 2250 us
  waiting for transfers between devices  1380 us (61%)
  matrix products  257 us (11%)
  local copies, waits for them, and re-layouts  225 us (10%)
  other arithmetic  176 us (8%)
  blocking collectives  163 us (7%)
    reduce_scatter x1, waiting for transfers between devices, reduce_grads(): lax.psum_scatter(grads[1], 'wsh', scatter_dimension=0, tiled=True)  652 us
    all_gather x1, waiting for transfers between devices, body(): lax.all_gather(in_weight, 'wsh', axis=0, tiled=True)  313 us
    reduce_scatter x1, waiting for transfers between devices, reduce_grads(): lax.psum_scatter(grads[8], 'wsh', scatter_dimension=0, tiled=True)  253 us
    psum x1, waiting for transfers between devices, reduce_grads(): lax.psum((shares[0], shares[1], shares[2], shares[3], shares[4], shares[5...  163 us
    dot_general x12, matrix products, advance(): result = jnp.einsum('hts,shp->thp', mixing, x_block, precision=highest)  77.1 us
    another operation x42, other arithmetic  46.3 us
  transfers between devices with their start and end apart: 13, of which 4 were waited for; matrix products, arithmetic and copies ran while one was open for 14% of the time, Pallas kernels for 0%

commit v1 on v0

--- a/solution.py
+++ b/solution.py
@@ -9,6 +9,27 @@
 CONVC = 3328
 epsilon = 1e-05
 highest = lax.Precision.HIGHEST
+
+
+def ring_gather(shard, axis, dim):
+    length, here, extent = (lax.axis_size(axis), lax.axis_index(axis), shard.shape[dim])
+    right = [(i, (i + 1) % length) for i in range(length)]
+    left = [(i, (i - 1) % length) for i in range(length)]
+    out = jnp.zeros((*shard.shape[:dim], length * extent, *shard.shape[dim + 1 :]), shard.dtype)
+    out = lax.dynamic_update_slice_in_dim(out, shard, here * extent, axis=dim)
+    from_left = from_right = shard
+    half = length // 2
+    for step in range(1, half + 1):
+        from_left = lax.ppermute(from_left, axis, right)
+        out = lax.dynamic_update_slice_in_dim(
+            out, from_left, (here - step) % length * extent, axis=dim
+        )
+        if step < length - half:
+            from_right = lax.ppermute(from_right, axis, left)
+            out = lax.dynamic_update_slice_in_dim(
+                out, from_right, (here + step) % length * extent, axis=dim
+            )
+    return out
 
 
 def shifted(block, axis, distance):
@@ -126,7 +147,7 @@
 ):
     gathered = (
         lax.all_gather(norm_gain, "wsh", axis=0, tiled=True),
-        lax.all_gather(in_weight, "wsh", axis=0, tiled=True),
+        ring_gather(in_weight, "wsh", 0),
         lax.all_gather(conv_weight, "wsh", axis=0, tiled=True),
         lax.all_gather(conv_bias, "wsh", axis=0, tiled=True),
         lax.all_gather(dt_bias, "wsh", axis=0, tiled=True),

time: 2260 us -> 2380 us (1.053)
  blocking collectives: 163 us -> 498 us
  waiting for transfers between devices: 1380 us -> 1170 us
    all_gather x1, blocking collectives: 13.6 us -> 368 us  [body(): lax.all_gather(norm_gain, 'wsh', axis=0, tiled=True)]
    all_gather x1 -> x0, waiting for transfers between devices: 313 us -> none  [body(): lax.all_gather(in_weight, 'wsh', axis=0, tiled=True)]
    ppermute x0 -> x3, waiting for transfers between devices: none -> 108 us  [the longest x2 108 us: ring_gather(): from_left = lax.ppermute(from_left, axis, right)]
  transfers between devices with their start and end apart: 13 -> 15, of which waited for: 4 -> 4; matrix products, arithmetic and copies ran while one was open for 14% -> 15% of each run, Pallas kernels for 0% -> 0%
where the time goes in v1:
time: 2380 us; the launch traced here: 2360 us
  waiting for transfers between devices  1170 us (49%)
  blocking collectives  498 us (21%)
  matrix products  242 us (10%)
  local copies, waits for them, and re-layouts  216 us (9%)
  other arithmetic  182 us (8%)
  starting transfers between devices  27.2 us (1%)
    reduce_scatter x1, waiting for transfers between devices, reduce_grads(): lax.psum_scatter(grads[1], 'wsh', scatter_dimension=0, tiled=True)  652 us
    all_gather x1, blocking collectives, body(): lax.all_gather(norm_gain, 'wsh', axis=0, tiled=True)  368 us
    reduce_scatter x1, waiting for transfers between devices, reduce_grads(): lax.psum_scatter(grads[8], 'wsh', scatter_dimension=0, tiled=True)  251 us
    psum x1, waiting for transfers between devices, reduce_grads(): lax.psum((shares[0], shares[1], shares[2], shares[3], shares[4], shares[5...  163 us
    ppermute x2, waiting for transfers between devices, ring_gather(): from_left = lax.ppermute(from_left, axis, right)  108 us
    dot_general x12, matrix products, advance(): result = jnp.einsum('hts,shp->thp', mixing, x_block, precision=highest)  78.4 us
    another operation x73, local copies, waits for them, and re-layouts  56.5 us
    another operation x42, other arithmetic  49 us
  transfers between devices with their start and end apart: 15, of which 4 were waited for; matrix products, arithmetic and copies ran while one was open for 15% of the time, Pallas kernels for 0%

profile of v1, /device:TPU:0, one launch (start us, length us, event | category | flops | bytes accessed | tf_op | source)
XLA Modules:
  0.0 2360.2 jit_solution(4153259348875429102)
XLA Ops:
  7.2 3.1 collective-permute-start
  12.4 108.0 %collective-permute-done = bf16[384,6448]{0,1:T(8,128)(2,1)} collective-permute-done((bf16[384,6448]{0,1:T(8,128)(2,1)}, bf16[384,6448]{0,1:T(8,128)(2,1)}, u32[]{:S(2)}, u32[]{:S(2)}) %collective-permute-start) | collective-permute-done | bytes 4952096 | tf_op jit(solution)/shard_map/ppermute | solution.py:23
  121.2 367.8 %all-gather = bf16[4,1,384]{2,1,0:T(2,128)(2,1)S(1)} all-gather(bf16[1,1,384]{2,1,0:T(2,128)(2,1)S(1)} %reshape.477), channel_id=1, replica_groups=mesh['seq'=4,'grp'=2,'wsh'=4] {'wsh'}, dimensions={0}, use_global_device_ids=true | all-gather | bytes 3840 | tf_op jit(solution)/shard_map/all_gather | solution.py:149
  492.1 13.2 all-gather.1
  506.8 3.4 constant_dynamic-update-slice_fusion.6
  510.3 3.4 constant_dynamic-update-slice_fusion.5
  513.8 3.4 constant_dynamic-update-slice_fusion.4
  517.2 3.5 constant_dynamic-update-slice_fusion.3
  520.8 6.4 convolution_convert_fusion
  530.5 3.4 collective-permute-start.3
  537.0 10.9 all-reduce.25
  549.8 3.6 all-to-all-start
  556.4 6.9 multiply_convert_fusion
  564.6 4.4 all-to-all-start.1
  571.3 16.7 all_gather.32
  593.8 79.0 %while.86 = (s32[]{:T(128)}, f32[12,128,64]{1,2,0:T(8,128)S(1)}, f32[4,256,12,64]{1,3,2,0:T(8,128)}, f32[4,256,12]{1,2,0:T(8,128)}, f32[4,256,12]{1,2,0:T(8,128)...) while((s32[]{:T(128)}, f32[12,128,64]{1,2,0:T(8,128)S(1)}, ...), condition=%wide.region_4.5_spmd.clone.clone, body=%wide.region_1.4_spmd.clone.clone.sunk | while | flops 1313970176 | bytes 7890463 | solution.py:100
  606.4 5.5 fusion.259
  626.2 5.5 fusion.259
  645.9 5.5 fusion.259
  665.7 5.5 fusion.259
  672.9 3.9 fusion.162
  676.8 4.7 all-to-all-start.2
  681.7 13.7 all-gather.2
  695.4 4.6 multiply_reduce_fusion.7
  700.6 8.7 multiply_reduce_fusion.4
  709.3 5.1 fusion.160
  714.4 4.4 all-to-all-start.3
  725.0 124.5 %while.87 = (s32[]{:T(128)}, f32[12,128,64]{1,2,0:T(8,128)}, f32[4,128,256]{1,2,0:T(8,128)}, f32[4,12,256,256]{3,2,1,0:T(8,128)}, f32[4,1,256,256]{3,2,1,0:T(8,1...) while((s32[]{:T(128)}, f32[12,128,64]{1,2,0:T(8,128)}, ...), condition=%wide.region_10.11_spmd.clone.clone, body=%wide.region_7.10_spmd.clone.clone.sunk | while | flops 709793792 | bytes 22276536 | solution.py:100
  736.4 5.2 multiply_dynamic-update-slice_fusion.3
  766.8 5.3 multiply_dynamic-update-slice_fusion.3
  798.2 5.1 multiply_dynamic-update-slice_fusion.3
  829.5 5.3 multiply_dynamic-update-slice_fusion.3
  849.5 3.3 convert_element_type.189
  857.7 236.7 %while.88 = (s32[]{:T(128)}, f32[12,128,64]{1,2,0:T(8,128)S(1)}, f32[4,256,12,64]{1,3,2,0:T(8,128)}, f32[4,256,12]{1,2,0:T(8,128)}, f32[4,256,12]{1,2,0:T(8,128)...) while((s32[]{:T(128)}, f32[12,128,64]{1,2,0:T(8,128)S(1)}, ...), condition=%wide.region_21.22_spmd.clone.clone, body=%wide.region_11.21_spmd.clone.clone.sunk | while | flops 2628807680 | bytes 44792864 | solution.py:100
  869.4 9.3 fusion.282
  889.7 3.2 reduce-window.64
  909.6 4.9 fusion.281
  928.5 9.3 fusion.282
  948.8 3.2 reduce-window.64
  968.6 4.9 fusion.281
  987.6 9.3 fusion.282
  1007.9 3.2 reduce-window.64
  1027.8 4.8 fusion.281
  1046.6 9.3 fusion.282
  1067.0 3.2 reduce-window.64
  1086.8 4.9 fusion.281
  1101.1 9.4 fusion.176
  1111.1 2.9 fusion.161
  1114.0 20.4 all_to_all.69
  1136.4 12.2 multiply_reduce_fusion.3
  1151.0 4.2 pad_add_fusion
  1161.7 9.2 all_to_all.70
  1172.2 5.0 fusion.154
  1177.2 19.0 fusion.173
  1198.2 251.2 %reduce-scatter.11.cloned.1.call-done = f32[768,1536]{1,0:T(8,128)} async-done(((f32[3072,1536]{1,0:T(8,128)}), f32[768,1536]{1,0:T(8,128)}) %reduce-scatter.11.cloned.1.call-update) | async-done | bytes 4718608 | tf_op jit(solution)/shard_map/reduce_scatter | solution.py:117
  1449.4 651.6 %reduce-scatter.9.cloned.1.call-done = f32[384,6448]{0,1:T(8,128)} async-done(((f32[1536,6448]{0,1:T(8,128)}), f32[384,6448]{0,1:T(8,128)}) %reduce-scatter.9.cloned.1.call-update) | async-done | bytes 9904144 | tf_op jit(solution)/shard_map/reduce_scatter | solution.py:110
  2103.7 7.4 fusion.164
  2111.1 2.7 multiply_reduce_fusion.5
  2114.9 14.0 fusion.168
  2128.9 21.3 all-reduce.24
  2150.7 2.8 fusion.175
  2154.6 24.8 %all-reduce.22 = (f32[384]{0:T(512)}, f32[832,4]{0,1:T(4,128)}, f32[832]{0:T(1024)}, f32[12]{0:T(128)}, f32[12]{0:T(128)}, /*index=5*/f32[12]{0:T(128)}, f32[768]{0:T(1024)}) all-reduce(f32[384]{0:T(512)S(1)} %dynamic-slice.5, f32[832,4]{0,1:T(4,128)S(1)} %copy.193, ...), channel_id=1, replica_groups=mesh['seq'=4,'grp'=2,'wsh'=4] {'seq','grp'}, use_global_device_ids=true, to_apply=%region_26.27 | all-reduce | flops 5348 | bytes 42784 | tf_op jit(solution)/shard_map/psum | solution.py:119
  2179.4 163.0 %all-reduce.28.cloned.1.call-done = (f32[384,6448]{0,1:T(8,128)}, f32[768,1536]{1,0:T(8,128)}) async-done(((f32[384,6448]{0,1:T(8,128)}, f32[768,1536]{1,0:T(8,128)}), (f32[384,6448]{0,1:T(8,128)}, f32[768,1536]{1,0:T(8,128)})) %all-reduce.28.cloned.1.call-update) | async-done | bytes 14622736 | tf_op jit(solution)/shard_map/psum | solution.py:119
  2342.4 8.5 copy.393
  (628 shorter events, 391.4 us)
Async XLA Ops:
  7.2 483.8 %copy-start.7 = (bf16[1,256,1536]{2,1,0:T(8,128)(2,1)S(1)}, bf16[1,256,1536]{2,1,0:T(8,128)(2,1)}, u32[]{:S(2)}) copy-start(bf16[1,256,1536]{2,1,0:T(8,128)(2,1)} %param.17) | copy-start | bytes 2359300
  7.2 484.9 %copy-start.47 = (bf16[832,4]{0,1:T(4,128)(2,1)S(1)}, bf16[832,4]{0,1:T(4,128)(2,1)}, u32[]{:S(2)}) copy-start(bf16[832,4]{0,1:T(4,128)(2,1)} %param.20) | copy-start | bytes 19972
  7.2 693.3 %all-gather.5.cloned.1.call-start = ((), (), s32[]{:S(2)}) async-start(), calls=%async_computation.10 | async-start | bytes 11796480 | tf_op jit(solution)/shard_map/all_gather | solution.py:193
  7.2 113.2 %collective-permute-start = (bf16[384,6448]{0,1:T(8,128)(2,1)}, bf16[384,6448]{0,1:T(8,128)(2,1)}, u32[]{:S(2)}, u32[]{:S(2)}) collective-permute-start(bf16[384,6448]{0,1:T(8,128)(2,1)} %param.19), channel_id=1, source_target_pairs={{0,1},{1,2},{2,3},{3,0},{4,5},{5,6},{6,7},{7,4},{8,9},{9,10},{10,1... | collective-permute-start | bytes 14856200 | tf_op jit(solution)/shard_map/ppermute | solution.py:23
  10.3 503.4 %collective-permute-start.1 = (bf16[384,6448]{0,1:T(8,128)(2,1)}, bf16[384,6448]{0,1:T(8,128)(2,1)}, u32[]{:S(2)}, u32[]{:S(2)}) collective-permute-start(bf16[384,6448]{0,1:T(8,128)(2,1)} %param.19), channel_id=1, source_target_pairs={{0,3},{1,0},{2,1},{3,2},{4,7},{5,4},{6,5},{7,6},{8,11},{9,8},{10,9... | collective-permute-start | bytes 14856200 | tf_op jit(solution)/shard_map/ppermute | solution.py:28
  120.4 396.8 %collective-permute-start.2 = (bf16[384,6448]{0,1:T(8,128)(2,1)}, bf16[384,6448]{0,1:T(8,128)(2,1)}, u32[]{:S(2)}, u32[]{:S(2)}) collective-permute-start(bf16[384,6448]{0,1:T(8,128)(2,1)} %collective-permute-done), channel_id=1, source_target_pairs={{0,1},{1,2},{2,3},{3,0},{4,5},{5,6},{6,7},{7,4},{8,9},{9,10},{10,1... | collective-permute-start | bytes 14856200 | tf_op jit(solution)/shard_map/ppermute | solution.py:23
  489.0 17.9 copy-start.31
  490.9 14.3 copy-start.43
  520.8 6.7 copy-start.5
  520.8 13.3 copy-start.52
  520.8 15.2 copy-start.57
  520.8 15.4 copy-start.58
  520.8 15.7 copy-start.59
  520.8 15.9 copy-start.53
  527.5 22.3 copy-start.9
  530.5 22.9 collective-permute-start.3
  534.0 22.4 copy-start.23
  534.0 22.4 copy-start.25
  534.0 22.4 copy-start.27
  534.1 22.4 copy-start.29
  549.8 14.8 all-to-all-start
  556.4 7.0 copy-start
  564.6 25.5 %all-to-all-start.1 = ((bf16[256,4,768]{0,2,1:T(8,128)(2,1)}), bf16[256,4,768]{0,2,1:T(8,128)(2,1)}, u32[]{:S(2)}, u32[]{:S(2)}) async-start(bf16[256,4,768]{0,2,1:T(8,128)(2,1)} %bitcast.6), calls=%async_computation.1 | async-start | bytes 3145728 | tf_op jit(solution)/shard_map/all_to_all | solution.py:175
  676.8 18.5 all-to-all-start.2
  695.3 14.0 copy-start.17
  700.5 8.8 copy-start.37
  700.5 8.8 copy-start.46
  700.5 8.8 copy-start.3
  714.4 135.0 %all-to-all-start.3 = ((bf16[256,4,768]{0,2,1:T(8,128)(2,1)}), bf16[256,4,768]{0,2,1:T(8,128)(2,1)}, u32[]{:S(2)}, u32[]{:S(2)}) async-start(bf16[256,4,768]{0,2,1:T(8,128)(2,1)} %bitcast.595), calls=%async_computation.3 | async-start | bytes 3145728 | tf_op jit(solution)/shard_map/all_to_all | solution.py:210
  718.8 417.5 %reduce-scatter.7.cloned.1.call-start = ((), (), s32[]{:S(2)}) async-start(), calls=%async_computation.11 | async-start | bytes 1310720 | tf_op jit(solution)/shard_map/reduce_scatter | solution.py:217
  772.1 5.6 copy-start.34
  772.1 5.6 copy-start.13
  803.4 5.6 copy-start.34
  803.4 5.6 copy-start.13
  834.8 5.5 copy-start.13
  897.2 12.3 copy-start.1
  897.2 12.3 copy-start.2
  956.3 12.3 copy-start.1
  956.3 12.3 copy-start.2
  1015.4 12.4 copy-start.1
  1015.4 12.4 copy-start.2
  1074.5 12.4 copy-start.1
  1074.5 12.4 copy-start.2
  1094.4 6.7 copy-start.4
  1094.4 6.7 copy-start.18
  1094.4 6.7 copy-start.38
  1101.0 348.4 %reduce-scatter.11.cloned.1.call-start = ((), (), s32[]{:S(2)}) async-start(), calls=%async_computation.13 | async-start | bytes 23592960 | tf_op jit(solution)/shard_map/reduce_scatter | solution.py:117
  1110.5 990.6 %reduce-scatter.9.cloned.1.call-start = ((), (), s32[]{:S(2)}) async-start(), calls=%async_computation.12 | async-start | bytes 49520640 | tf_op jit(solution)/shard_map/reduce_scatter | solution.py:110
  1136.3 12.2 copy-start.24
  1136.4 12.2 copy-start.26
  1136.4 12.2 copy-start.28
  1136.4 12.3 copy-start.30
  1151.0 10.4 copy-start.20
  1151.0 10.4 copy-start.21
  1151.0 10.4 copy-start.22
  1151.0 10.4 copy-start.49
  1151.0 10.4 copy-start.51
  1160.1 10.8 collective-permute-start.4
  1196.2 957.2 %reduce-scatter.13.cloned.1.call-start = ((), (), s32[]{:S(2)}) async-start(), calls=%async_computation.14 | async-start | bytes 2129920
  1198.2 1144.3 %all-reduce.28.cloned.1.call-start = ((), (), s32[]{:S(2)}) async-start(), calls=%async_computation.15 | async-start | bytes 29245440 | tf_op jit(solution)/shard_map/psum | solution.py:119
  2114.9 14.0 copy-start.40
  2114.9 35.8 %copy-start.42 = (f32[256]{0:T(256)S(1)}, f32[256]{0:T(256)}, u32[]{:S(2)}) copy-start(f32[256]{0:T(256)} %copy-done.41) | copy-start | bytes 3076
  2114.9 35.8 %copy-start.15 = (bf16[1,256,1536]{2,1,0:T(8,128)(2,1)S(1)}, bf16[1,256,1536]{2,1,0:T(8,128)(2,1)}, u32[]{:S(2)}) copy-start(bf16[1,256,1536]{2,1,0:T(8,128)(2,1)} %param.27) | copy-start | bytes 2359300
  2342.4 8.5 copy-start.12
  (35 other events, 118.1 us)
Sparse Core Ops, SparseCore 0:
  120.5 363.3 all-gather.4
  1101.1 33.5 reduce-scatter.6
  1137.1 312.3 reduce-scatter.10
  1451.7 649.3 reduce-scatter.8
  2103.8 40.4 reduce-scatter.12
  2147.9 194.4 all-reduce.27
